TPU v7x, 256 devices: a whole 4x4x8 slice. The times are simulated.
256 devices in a mesh: dp: 16 (over x_lo, y, core), mp: 8 (over z), side: 2 (over x_hi).
Axes of the slice: x: 4 (x_hi: 2, x_lo: 2; x = x_hi * 2 + x_lo), y: 4, z: 8, core: 2. Of those that a mesh axis runs over, the one named last changes fastest.
Arguments:
- tokens: bfloat16 [4096, 3072], P('dp', 'mp'), may hold values from -6 to 6
- up_weight: bfloat16 [2, 3072, 6144], P('side', 'dp', 'mp'), may hold values from -0.109375 to 0.109375
- down_weight: bfloat16 [2, 6144, 3072], P('side', 'mp', 'dp'), may hold values from -0.078125 to 0.078125
- mod_table: float32 [2, 50, 3, 3072], P('side'), may hold values from -3 to 3
- timesteps: int32 [16], P('dp'), may hold values from 0 to 49
- valid_counts: int32 [16], replicated, may hold values from 64 to 256, as said below
Outputs:
- block_out: bfloat16 [2, 4096, 3072], P('side', 'dp', 'mp')
- up_grads: float32 [3072, 6144], P(('dp', 'side'), 'mp')
- down_grads: float32 [6144, 3072], P('mp', ('dp', 'side'))
Inputs may be any that keep to these rules, and one draw needn't show every extreme that they name: `valid_counts`: every image has at least 64 valid tokens, and in every draw some image has all 256 valid.
All inputs are finite; a program needn't handle non-finite values.
Results may differ from a plain program's by a relative error of at most 0.018.
Values may be sent and summed in bfloat16 or wider, within the bound.
A program may use at most 64 MiB of HBM per device.

v0:
```python
import jax
import jax.numpy as jnp
from jax import lax
from jax.sharding import PartitionSpec as P


def passed_along(x, axis, by):
    peers = lax.axis_size(axis)
    pairs = [(i, i + by) for i in range(peers) if 0 <= i + by < peers]
    return lax.ppermute(x, axis, pairs)


def gelu_tanh(values):
    return jax.nn.gelu(values, approximate=True)


def shards(tokens, up_weight, down_weight, mod_table, timesteps, valid_counts):
    gathered = lax.all_gather(tokens, "mp", axis=1, tiled=True)
    width = gathered.shape[1]
    shard_width = tokens.shape[1]
    mp_offset = lax.axis_index("mp") * shard_width
    is_student = lax.axis_index("side") == 1
    wide = gathered.astype(jnp.float32)
    average = jnp.mean(wide, axis=-1, keepdims=True)
    centred = wide - average
    variance = jnp.mean(centred * centred, axis=-1, keepdims=True)
    scaled = centred * lax.rsqrt(variance + 1e-06)
    plan = mod_table.shape[1]
    one_hot = (jnp.arange(plan, dtype=jnp.int32)[None, :] == timesteps[0]).astype(jnp.float32)
    modulation = jnp.dot(
        one_hot,
        mod_table[0].reshape(plan, 3 * width),
        precision=lax.Precision.HIGHEST,
        preferred_element_type=jnp.float32,
    ).reshape(3, width)
    normed = (scaled * (1.0 + modulation[1]) + modulation[0]).astype(jnp.bfloat16)
    gate_row = modulation[2]
    hidden_pre = jnp.dot(
        normed,
        lax.all_gather(up_weight[0], "dp", axis=0, tiled=True),
        preferred_element_type=jnp.float32,
    )
    hidden_act = gelu_tanh(hidden_pre).astype(jnp.bfloat16)
    down_full = lax.all_gather(down_weight[0], "dp", axis=1, tiled=True)
    partial_value = jnp.dot(hidden_act, down_full, preferred_element_type=jnp.float32)
    positions = jnp.arange(normed.shape[0], dtype=jnp.int32)
    own_count = lax.dynamic_index_in_dim(valid_counts, lax.axis_index("dp"), 0, keepdims=False)
    valid_col = (positions < own_count).astype(jnp.float32)[:, None]
    valid_total = jnp.sum(valid_counts).astype(jnp.float32)
    mixed = lax.psum(partial_value.astype(jnp.bfloat16), "mp").astype(jnp.float32)
    out_full = (wide + gate_row * mixed).astype(jnp.bfloat16)
    out_local = lax.dynamic_slice_in_dim(out_full, mp_offset, shard_width, 1)
    other_full = passed_along(out_full, "side", 1)
    differ = out_full.astype(jnp.float32) - other_full.astype(jnp.float32)
    grad_out = (gate_row * differ * valid_col / jnp.sqrt(valid_total)).astype(jnp.bfloat16)

    def backprop():
        grad_act = lax.dot_general(
            grad_out, down_full, (((1,), (1,)), ((), ())), preferred_element_type=jnp.float32
        )
        unused, pullback = jax.vjp(gelu_tanh, hidden_pre)
        return pullback(grad_act)[0].astype(jnp.bfloat16)

    def no_backprop():
        return jnp.zeros(hidden_pre.shape, jnp.bfloat16)

    grad_pre = lax.cond(is_student, backprop, no_backprop)
    ff_width = hidden_act.shape[1]

    def product():
        return lax.dot_general(
            normed, grad_pre, (((0,), (0,)), ((), ())), preferred_element_type=jnp.float32
        )

    def nothing():
        return jnp.zeros(
            (width // lax.axis_size(("dp", "side")) * lax.axis_size(("dp", "side")), ff_width),
            jnp.float32,
        )

    up_share = lax.psum_scatter(
        lax.cond(is_student, product, nothing).astype(jnp.bfloat16),
        ("dp", "side"),
        scatter_dimension=0,
        tiled=True,
    ).astype(jnp.float32)

    def down_product():
        return lax.dot_general(
            hidden_act, grad_out, (((0,), (0,)), ((), ())), preferred_element_type=jnp.float32
        )

    def down_nothing():
        return jnp.zeros((ff_width, width), jnp.float32)

    down_term = lax.cond(is_student, down_product, down_nothing)
    down_share = lax.psum_scatter(
        down_term.astype(jnp.bfloat16), ("dp", "side"), scatter_dimension=1, tiled=True
    ).astype(jnp.float32)
    return (out_local[None], up_share, down_share)


def solution(mesh):
    placed = (
        P("dp", "mp"),
        P("side", "dp", "mp"),
        P("side", "mp", "dp"),
        P("side", None, None, None),
        P("dp"),
        P(),
    )
    return jax.shard_map(
        shards,
        mesh=mesh,
        in_specs=placed,
        out_specs=(P("side", "dp", "mp"), P(("dp", "side"), "mp"), P("mp", ("dp", "side"))),
        check_vma=False,
    )
```

profile of v0, /device:TPU:1, one launch (start us, length us, event | category | flops | bytes accessed | tf_op | source)
XLA Modules:
  0.0 593.4 jit_solution(2284106600337096998)
XLA Ops:
  9.4 6.5 %reduce = f32[50,3,3072]{2,1,0:T(4,128)S(1)} reduce(f32[1,50,3,3072]{3,0,2,1:T(1,128)} %param.15, f32[]{:T(128)} %constant.65), dimensions={0}, to_apply=%param.15.reduce_sub_computation | reduce | bytes 3686404 | tf_op args[3]
  16.5 1.2 copy.14
  19.1 29.2 %all-gather.6.cloned.1.call-done = bf16[256,3072]{1,0:T(8,128)(2,1)} async-done(((bf16[256,384]{1,0:T(8,128)(2,1)}), bf16[256,3072]{1,0:T(8,128)(2,1)}) %all-gather.6.cloned.1.call-update) | async-done | bytes 1572880 | tf_op jit(solution)/shard_map/all_gather | solution.py:18
  48.2 1.8 convert_reduce_fusion
  50.1 2.0 fusion.11
  52.8 41.7 %all-gather.8.cloned.1.call-done = bf16[1,3072,768]{2,1,0:T(8,128)(2,1)} async-done(((bf16[1,192,768]{2,1,0:T(8,128)(2,1)}), bf16[1,3072,768]{2,1,0:T(8,128)(2,1)}) %all-gather.8.cloned.1.call-update) | async-done | bytes 4718608 | tf_op jit(solution)/shard_map/all_gather | solution.py:40
  94.5 4.6 fusion.23
  99.2 37.7 %all-gather.10.cloned.1.call-done = bf16[1,768,3072]{1,2,0:T(8,128)(2,1)} async-done(((bf16[1,768,192]{1,2,0:T(8,128)(2,1)}), bf16[1,768,3072]{1,2,0:T(8,128)(2,1)}) %all-gather.10.cloned.1.call-update) | async-done | bytes 4718608 | tf_op jit(solution)/shard_map/all_gather | solution.py:44
  136.9 4.9 convolution_convert_fusion
  142.1 74.3 %all-reduce.2.cloned.1.call-done = bf16[256,3072]{1,0:T(8,128)(2,1)} async-done(((bf16[256,3072]{1,0:T(8,128)(2,1)}), bf16[256,3072]{1,0:T(8,128)(2,1)}) %all-reduce.2.cloned.1.call-update) | async-done | bytes 1572880 | tf_op jit(solution)/shard_map/psum | solution.py:50
  216.3 3.1 fusion.15
  219.5 5.8 collective-permute-start
  227.8 25.6 %collective-permute-done = bf16[256,3072]{1,0:T(8,128)(2,1)} collective-permute-done((bf16[256,3072]{1,0:T(8,128)(2,1)}, bf16[256,3072]{1,0:T(8,128)(2,1)}, u32[]{:S(2)}, u32[]{:S(2)}) %collective-permute-start) | collective-permute-done | bytes 1572896 | tf_op jit(solution)/shard_map/ppermute | solution.py:10
  253.4 2.6 divide_convert_fusion
  256.1 2.5 conditional.4
  256.1 2.5 broadcast.75
  259.6 2.8 conditional.5
  259.6 2.8 broadcast.76
  262.4 6.6 %copy.12 = bf16[768,3072]{0,1:T(8,128)(2,1)} copy(bf16[768,3072]{1,0:T(8,128)(2,1)} %get-tuple-element.43) | data formatting | bytes 9437184 | tf_op jit(solution)/shard_map/cond | solution.py:96
  269.0 1.6 dynamic-slice_bitcast_fusion
  270.6 155.2 %reduce-scatter.3.cloned.1.call-done = bf16[96,768]{1,0:T(8,128)(2,1)} async-done(((bf16[3072,768]{1,0:T(8,128)(2,1)}), bf16[96,768]{1,0:T(8,128)(2,1)}) %reduce-scatter.3.cloned.1.call-update) | async-done | bytes 147472 | tf_op jit(solution)/shard_map/reduce_scatter | solution.py:81
  425.9 1.6 convert_element_type.71
  427.5 157.4 %reduce-scatter.5.cloned.1.call-done = bf16[768,96]{0,1:T(8,128)(2,1)} async-done(((bf16[768,3072]{0,1:T(8,128)(2,1)}), bf16[768,96]{0,1:T(8,128)(2,1)}) %reduce-scatter.5.cloned.1.call-update) | async-done | bytes 147472 | tf_op jit(solution)/shard_map/reduce_scatter | solution.py:97
  584.9 1.6 convert_element_type.73
  (31 shorter events, 7.5 us)
Async XLA Ops:
  7.2 41.1 %all-gather.6.cloned.1.call-start = ((), (), s32[]{:S(2)}) async-start(), calls=%async_computation.2 | async-start | bytes 1769472 | tf_op jit(solution)/shard_map/all_gather | solution.py:18
  7.9 86.6 %all-gather.8.cloned.1.call-start = ((), (), s32[]{:S(2)}) async-start(), calls=%async_computation.6 | async-start | bytes 5013504 | tf_op jit(solution)/shard_map/all_gather | solution.py:40
  8.6 128.2 %all-gather.10.cloned.1.call-start = ((), (), s32[]{:S(2)}) async-start(), calls=%async_computation.7 | async-start | bytes 5013504 | tf_op jit(solution)/shard_map/all_gather | solution.py:44
  9.4 207.0 %all-reduce.2.cloned.1.call-start = ((), (), s32[]{:S(2)}) async-start(), calls=%async_computation.3 | async-start | bytes 3145728 | tf_op jit(solution)/shard_map/psum | solution.py:50
  48.2 3.8 copy-start
  99.2 42.7 %copy-start.1 = (bf16[256,768]{1,0:T(8,128)(2,1)}, bf16[256,768]{1,0:T(8,128)(2,1)S(1)}, u32[]{:S(2)}) copy-start(bf16[256,768]{1,0:T(8,128)(2,1)S(1)} %get-tuple-element.39) | copy-start | bytes 1179652
  141.8 83.4 %copy-start.3 = (s32[16]{0:T(128)S(1)}, s32[16]{0:T(128)}, u32[]{:S(2)}) copy-start(s32[16]{0:T(128)} %param.17) | copy-start | bytes 196
  141.8 284.0 %reduce-scatter.3.cloned.1.call-start = ((), (), s32[]{:S(2)}) async-start(), calls=%async_computation.4 | async-start | bytes 4866048 | tf_op jit(solution)/shard_map/reduce_scatter | solution.py:81
  219.5 34.0 %collective-permute-start = (bf16[256,3072]{1,0:T(8,128)(2,1)}, bf16[256,3072]{1,0:T(8,128)(2,1)}, u32[]{:S(2)}, u32[]{:S(2)}) collective-permute-start(bf16[256,3072]{1,0:T(8,128)(2,1)} %fusion.15), channel_id=1, source_target_pairs={{0,1},{2,3},{4,5},{6,7},{8,9},{10,11},{12,13},{14,15},{16,17},{18,... | collective-permute-start | bytes 4718600 | tf_op jit(solution)/shard_map/ppermute | solution.py:10
  258.6 1.0 copy-start.2
  258.6 326.3 %reduce-scatter.5.cloned.1.call-start = ((), (), s32[]{:S(2)}) async-start(), calls=%async_computation.5 | async-start | bytes 4866048 | tf_op jit(solution)/shard_map/reduce_scatter | solution.py:97
Sparse Core Ops, SparseCore 0:
  9.8 38.4 all-gather.5
  50.1 44.3 all-gather.7
  96.4 40.4 all-gather.9
  142.0 74.3 all-reduce.1
  258.7 167.0 reduce-scatter.2
  428.2 156.6 reduce-scatter.4
where the time goes:
time: 594 us; the launch traced here: 593 us
  waiting for transfers between devices  523 us (88%)
  other arithmetic  21.3 us (4%)
  local copies, waits for them, and re-layouts  16.8 us (3%)
  between operations  15.5 us (3%)
  matrix products  10.3 us (2%)
  starting transfers between devices  6.19 us (1%)
    reduce_scatter x1, waiting for transfers between devices, shards(): lax.psum_scatter(down_term.astype(jnp.bfloat16), ('dp', 'side'), scatter_...  157 us
    reduce_scatter x1, waiting for transfers between devices, shards(): lax.psum_scatter(lax.cond(is_student, product, nothing).astype(jnp.bfloat...  155 us
    psum x1, waiting for transfers between devices, shards(): lax.psum(partial_value.astype(jnp.bfloat16), 'mp').astype(jnp.float32)  74.3 us
    all_gather x1, waiting for transfers between devices, shards(): lax.all_gather(up_weight[0], 'dp', axis=0, tiled=True)  41.7 us
    all_gather x1, waiting for transfers between devices, shards(): down_full = lax.all_gather(down_weight[0], 'dp', axis=1, tiled=True)  37.7 us
    all_gather x1, waiting for transfers between devices, shards(): gathered = lax.all_gather(tokens, 'mp', axis=1, tiled=True)  29.2 us
    ppermute x1, waiting for transfers between devices, passed_along(): return lax.ppermute(x, axis, pairs)  25.6 us
  transfers between devices with their start and end apart: 7, of which 7 were waited for; matrix products, arithmetic and copies ran while one was open for 6% of the time, Pallas kernels for 0%

commit v1 on v0

--- a/solution.py
+++ b/solution.py
@@ -1,7 +1,23 @@
+import functools
 import jax
 import jax.numpy as jnp
 from jax import lax
 from jax.sharding import PartitionSpec as P
+
+
+def supply_seats_all_now(arr_in, along_dim):
+    return jnp.concatenate(
+        lax.all_to_all(
+            jnp.stack(lax.psum(1, axis_name="dp") * [arr_in]),
+            axis_name="dp",
+            split_axis=0,
+            concat_axis=0,
+        ),
+        axis=along_dim,
+    )
+
+
+_manage_knots = functools.partial(supply_seats_all_now, along_dim=1)
 
 
 def passed_along(x, axis, by):
@@ -41,7 +57,7 @@
         preferred_element_type=jnp.float32,
     )
     hidden_act = gelu_tanh(hidden_pre).astype(jnp.bfloat16)
-    down_full = lax.all_gather(down_weight[0], "dp", axis=1, tiled=True)
+    down_full = _manage_knots(down_weight[0])
     partial_value = jnp.dot(hidden_act, down_full, preferred_element_type=jnp.float32)
     positions = jnp.arange(normed.shape[0], dtype=jnp.int32)
     own_count = lax.dynamic_index_in_dim(valid_counts, lax.axis_index("dp"), 0, keepdims=False)

time: 594 us -> 573 us (0.965)
  waiting for transfers between devices: 523 us -> 492 us
  starting transfers between devices: 6.19 us -> 13.6 us
    all_gather x1 -> x0, waiting for transfers between devices: 37.7 us -> none  [shards(): down_full = lax.all_gather(down_weight[0], 'dp', axis=1, tiled=True)]
    all_gather x1, waiting for transfers between devices: 41.7 us -> 53.2 us  [shards(): lax.all_gather(up_weight[0], 'dp', axis=0, tiled=True)]
    all_gather x1, waiting for transfers between devices: 29.2 us -> 19.7 us  [shards(): gathered = lax.all_gather(tokens, 'mp', axis=1, tiled=True)]
    all_to_all x0 -> x1, starting transfers between devices: none -> 7.5 us  [supply_seats_all_now(): lax.all_to_all(jnp.stack(lax.psum(1, axis_name='dp') * [arr_in]), axis_na...]
  transfers between devices with their start and end apart: 7 -> 7, of which waited for: 7 -> 6; matrix products, arithmetic and copies ran while one was open for 6% -> 6% of each run, Pallas kernels for 0% -> 0%
where the time goes in v1:
time: 573 us
  waiting for transfers between devices  492 us (86%)
  other arithmetic  21.3 us (4%)
  local copies, waits for them, and re-layouts  20.4 us (4%)
  between operations  15.2 us (3%)
  starting transfers between devices  13.6 us (2%)
  matrix products  10.5 us (2%)
    reduce_scatter x1, waiting for transfers between devices, shards(): lax.psum_scatter(down_term.astype(jnp.bfloat16), ('dp', 'side'), scatter_...  161 us
    reduce_scatter x1, waiting for transfers between devices, shards(): lax.psum_scatter(lax.cond(is_student, product, nothing).astype(jnp.bfloat...  155 us
    psum x1, waiting for transfers between devices, shards(): lax.psum(partial_value.astype(jnp.bfloat16), 'mp').astype(jnp.float32)  75.7 us
    all_gather x1, waiting for transfers between devices, shards(): lax.all_gather(up_weight[0], 'dp', axis=0, tiled=True)  53.2 us
    ppermute x1, waiting for transfers between devices, passed_along(): return lax.ppermute(x, axis, pairs)  25.6 us
    all_gather x1, waiting for transfers between devices, shards(): gathered = lax.all_gather(tokens, 'mp', axis=1, tiled=True)  19.7 us
  transfers between devices with their start and end apart: 7, of which 6 were waited for; matrix products, arithmetic and copies ran while one was open for 6% of the time, Pallas kernels for 0%

profile of v1, /device:TPU:1, one launch (start us, length us, event | category | flops | bytes accessed | tf_op | source)
XLA Modules:
  0.0 572.6 jit_solution(12400570121871779215)
XLA Ops:
  8.6 3.6 stack.3
  12.2 7.5 %all-to-all-start = ((bf16[16,768,192]{1,2,0:T(8,128)(2,1)}), bf16[16,768,192]{1,2,0:T(8,128)(2,1)}, u32[]{:S(2)}, u32[]{:S(2)}) async-start(bf16[16,768,192]{1,2,0:T(8,128)(2,1)} %stack.3), calls=%async_computation | async-start | bytes 9437184 | tf_op jit(solution)/shard_map/all_to_all | solution.py:10
  19.8 6.5 %reduce = f32[50,3,3072]{2,1,0:T(4,128)S(1)} reduce(f32[1,50,3,3072]{3,0,2,1:T(1,128)} %param.15, f32[]{:T(128)} %constant.65), dimensions={0}, to_apply=%param.15.reduce_sub_computation | reduce | bytes 3686404 | tf_op args[3]
  29.4 19.7 %all-gather.4.cloned.1.call-done = bf16[256,3072]{1,0:T(8,128)(2,1)} async-done(((bf16[256,384]{1,0:T(8,128)(2,1)}), bf16[256,3072]{1,0:T(8,128)(2,1)}) %all-gather.4.cloned.1.call-update) | async-done | bytes 1572880 | tf_op jit(solution)/shard_map/all_gather | solution.py:34
  49.2 1.8 convert_reduce_fusion
  51.0 2.0 fusion.11
  53.8 53.2 %all-gather.6.cloned.1.call-done = bf16[1,3072,768]{2,1,0:T(8,128)(2,1)} async-done(((bf16[1,192,768]{2,1,0:T(8,128)(2,1)}), bf16[1,3072,768]{2,1,0:T(8,128)(2,1)}) %all-gather.6.cloned.1.call-update) | async-done | bytes 4718608 | tf_op jit(solution)/shard_map/all_gather | solution.py:56
  107.0 4.6 fusion.23
  111.7 5.0 convolution_convert_fusion
  117.0 75.7 %all-reduce.2.cloned.1.call-done = bf16[256,3072]{1,0:T(8,128)(2,1)} async-done(((bf16[256,3072]{1,0:T(8,128)(2,1)}), bf16[256,3072]{1,0:T(8,128)(2,1)}) %all-reduce.2.cloned.1.call-update) | async-done | bytes 1572880 | tf_op jit(solution)/shard_map/psum | solution.py:66
  192.7 3.1 fusion.15
  195.8 5.8 %collective-permute-start = (bf16[256,3072]{1,0:T(8,128)(2,1)}, bf16[256,3072]{1,0:T(8,128)(2,1)}, u32[]{:S(2)}, u32[]{:S(2)}) collective-permute-start(bf16[256,3072]{1,0:T(8,128)(2,1)} %fusion.15), channel_id=1, source_target_pairs={{0,1},{2,3},{4,5},{6,7},{8,9},{10,11},{12,13},{14,15},{16,17},{18,... | collective-permute-start | bytes 4718600 | tf_op jit(solution)/shard_map/ppermute | solution.py:26
  204.1 25.6 %collective-permute-done = bf16[256,3072]{1,0:T(8,128)(2,1)} collective-permute-done((bf16[256,3072]{1,0:T(8,128)(2,1)}, bf16[256,3072]{1,0:T(8,128)(2,1)}, u32[]{:S(2)}, u32[]{:S(2)}) %collective-permute-start) | collective-permute-done | bytes 1572896 | tf_op jit(solution)/shard_map/ppermute | solution.py:26
  229.8 2.6 divide_convert_fusion
  232.4 2.5 conditional.4
  232.4 2.5 broadcast.76
  235.9 2.8 conditional.5
  235.9 2.8 broadcast.77
  238.7 6.6 %copy.12 = bf16[768,3072]{0,1:T(8,128)(2,1)} copy(bf16[768,3072]{1,0:T(8,128)(2,1)} %get-tuple-element.43) | data formatting | bytes 9437184 | tf_op jit(solution)/shard_map/cond | solution.py:112
  245.3 1.6 dynamic-slice_bitcast_fusion
  247.0 154.6 %reduce-scatter.3.cloned.1.call-done = bf16[96,768]{1,0:T(8,128)(2,1)} async-done(((bf16[3072,768]{1,0:T(8,128)(2,1)}), bf16[96,768]{1,0:T(8,128)(2,1)}) %reduce-scatter.3.cloned.1.call-update) | async-done | bytes 147472 | tf_op jit(solution)/shard_map/reduce_scatter | solution.py:97
  401.5 1.6 convert_element_type.71
  403.2 161.3 %reduce-scatter.5.cloned.1.call-done = bf16[768,96]{0,1:T(8,128)(2,1)} async-done(((bf16[768,3072]{0,1:T(8,128)(2,1)}), bf16[768,96]{0,1:T(8,128)(2,1)}) %reduce-scatter.5.cloned.1.call-update) | async-done | bytes 147472 | tf_op jit(solution)/shard_map/reduce_scatter | solution.py:113
  564.5 1.6 convert_element_type.73
  (31 shorter events, 7.9 us)
Async XLA Ops:
  7.2 42.0 %all-gather.4.cloned.1.call-start = ((), (), s32[]{:S(2)}) async-start(), calls=%async_computation.3 | async-start | bytes 1769472 | tf_op jit(solution)/shard_map/all_gather | solution.py:34
  7.9 99.1 %all-gather.6.cloned.1.call-start = ((), (), s32[]{:S(2)}) async-start(), calls=%async_computation.7 | async-start | bytes 5013504 | tf_op jit(solution)/shard_map/all_gather | solution.py:56
  12.2 99.4 %all-to-all-start = ((bf16[16,768,192]{1,2,0:T(8,128)(2,1)}), bf16[16,768,192]{1,2,0:T(8,128)(2,1)}, u32[]{:S(2)}, u32[]{:S(2)}) async-start(bf16[16,768,192]{1,2,0:T(8,128)(2,1)} %stack.3), calls=%async_computation | async-start | bytes 9437184 | tf_op jit(solution)/shard_map/all_to_all | solution.py:10
  19.7 172.9 %all-reduce.2.cloned.1.call-start = ((), (), s32[]{:S(2)}) async-start(), calls=%async_computation.4 | async-start | bytes 3145728 | tf_op jit(solution)/shard_map/psum | solution.py:66
  49.2 3.8 copy-start
  111.7 5.1 copy-start.1
  116.7 84.9 %copy-start.3 = (s32[16]{0:T(128)S(1)}, s32[16]{0:T(128)}, u32[]{:S(2)}) copy-start(s32[16]{0:T(128)} %param.17) | copy-start | bytes 196
  116.7 284.8 %reduce-scatter.3.cloned.1.call-start = ((), (), s32[]{:S(2)}) async-start(), calls=%async_computation.5 | async-start | bytes 4866048 | tf_op jit(solution)/shard_map/reduce_scatter | solution.py:97
  195.8 34.0 %collective-permute-start = (bf16[256,3072]{1,0:T(8,128)(2,1)}, bf16[256,3072]{1,0:T(8,128)(2,1)}, u32[]{:S(2)}, u32[]{:S(2)}) collective-permute-start(bf16[256,3072]{1,0:T(8,128)(2,1)} %fusion.15), channel_id=1, source_target_pairs={{0,1},{2,3},{4,5},{6,7},{8,9},{10,11},{12,13},{14,15},{16,17},{18,... | collective-permute-start | bytes 4718600 | tf_op jit(solution)/shard_map/ppermute | solution.py:26
  234.9 1.0 copy-start.2
  234.9 329.6 %reduce-scatter.5.cloned.1.call-start = ((), (), s32[]{:S(2)}) async-start(), calls=%async_computation.6 | async-start | bytes 4866048 | tf_op jit(solution)/shard_map/reduce_scatter | solution.py:113
Sparse Core Ops, SparseCore 0:
  9.8 39.3 all-gather.3
  51.0 55.9 all-gather.5
  116.9 75.7 all-reduce.1
  235.0 166.4 reduce-scatter.2
  403.9 160.5 reduce-scatter.4
